TPU v7x, 512 devices: a whole 4x4x16 slice. The times are simulated.
512 devices in a mesh: dp: 16 (over z), retr: 8 (over x, core), fsdp: 4 (over y).
Axes of the slice: x: 4, y: 4, z: 16, core: 2. Of those that a mesh axis runs over, the one named last changes fastest.
Arguments:
- queries: bfloat16 [65536, 2048], P(('dp', 'retr', 'fsdp')), may hold values from -110 to 110, as said below
- encodings: bfloat16 [2048, 128, 896], P(('dp', 'retr', 'fsdp')), may hold values from -6 to 6
- owner_ids: int32 [1024, 2], P(('dp', 'retr', 'fsdp')), may hold values from 0 to 7, all different within a row; in each aligned block of 2 rows (0 to 1, 2 to 3, ...) at most 2 rows name the same one
- local_ids: int32 [1024, 2], P(('dp', 'retr', 'fsdp')), may hold values from 0 to 3
- key_weight: bfloat16 [896, 2048], P(('dp', 'fsdp')), may hold values from -0.1875 to 0.1875
- value_weight: bfloat16 [896, 2048], P(('dp', 'fsdp')), may hold values from -0.1875 to 0.1875
Outputs:
- attended: bfloat16 [65536, 2048], P(('dp', 'retr', 'fsdp'))
Inputs may be any that keep to these rules, and one draw needn't show every extreme that they name: `queries`: entries are bounded. `owner_ids`: the two neighbours of a stretch have different owners; among the stretches of one device no owner is named more than 2 times, and in every draw some device's stretches name some owner exactly 2 times.
All inputs are finite; a program needn't handle non-finite values.
Results may differ from a plain program's by a relative error of at most 0.011.
Values may be sent and summed in bfloat16 or wider, within the bound.
No kernel may reach another device: no remote copies, remote signals or barrier semaphores. Data moves between devices by JAX's collectives and lax.ppermute only.
A program may use at most 64 MiB of HBM per device.

v0:
```python
import math
import jax
import jax.numpy as jnp
from jax import lax
from jax.sharding import PartitionSpec as P

HEADS = 16
STRETCH = 64


def passed_along(block, axis, distance):
    devices = range(lax.axis_size(axis))
    route = [(i - distance, i) for i in devices if i - distance in devices]
    return lax.ppermute(block, axis, route)


def body(queries, encodings, owner_ids, local_ids, key_weight, value_weight):
    tokens = queries.shape[0]
    columns = queries.shape[1]
    head_size = columns // HEADS
    stretches = tokens // STRETCH
    neighbours = owner_ids.shape[1]
    slot_count = stretches * neighbours
    owners = owner_ids.reshape(slot_count)
    places = local_ids.reshape(slot_count)
    gathered = lax.all_gather(encodings, "retr", axis=0, tiled=True)
    fetched = jnp.take(gathered, owners * encodings.shape[0] + places, axis=0)
    span = neighbours * encodings.shape[1]
    panel_rows = fetched.reshape(stretches * span, encodings.shape[2])
    key_full, value_full = (
        lax.all_gather(key_weight, ("dp", "fsdp"), axis=0, tiled=True),
        lax.all_gather(value_weight, ("dp", "fsdp"), axis=0, tiled=True),
    )
    prior_rows = passed_along(panel_rows[(stretches - 1) * span :], "fsdp", 1)
    every_row = jnp.concatenate([prior_rows, panel_rows], 0)
    key_block = jnp.dot(every_row, key_full, preferred_element_type=jnp.float32).astype(
        jnp.bfloat16
    )
    value_block = jnp.dot(every_row, value_full, preferred_element_type=jnp.float32).astype(
        jnp.bfloat16
    )
    key_block = key_block.reshape(stretches + 1, span, columns)
    value_block = value_block.reshape(stretches + 1, span, columns)
    padded = jnp.concatenate(
        [
            jnp.zeros((1, columns), jnp.bfloat16),
            queries,
            jnp.zeros((STRETCH - 1, columns), jnp.bfloat16),
        ],
        0,
    )
    query_block = padded.reshape(stretches + 1, STRETCH, HEADS, head_size)
    key_heads = key_block.reshape(stretches + 1, span, HEADS, head_size)
    value_heads = value_block.reshape(stretches + 1, span, HEADS, head_size)
    scores = jnp.einsum(
        "cqhd,ckhd->chqk", query_block, key_heads, preferred_element_type=jnp.float32
    ) / math.sqrt(head_size)
    probs = jax.nn.softmax(scores, axis=-1).astype(jnp.bfloat16)
    result = jnp.einsum(
        "chqk,ckhd->cqhd", probs, value_heads, preferred_element_type=jnp.float32
    ).astype(jnp.bfloat16)
    result = result.reshape((stretches + 1) * STRETCH, columns)[1 : tokens + 1]
    follower = lax.axis_index("fsdp") > 0
    position = jnp.arange(tokens, dtype=jnp.int32)
    visible = follower | (position >= STRETCH - 1)
    return jnp.where(visible[:, None], result, jnp.zeros_like(result))


def solution(mesh):
    in_specs = (
        P(("dp", "retr", "fsdp"), None),
        P(("dp", "retr", "fsdp"), None, None),
        P(("dp", "retr", "fsdp"), None),
        P(("dp", "retr", "fsdp"), None),
        P(("dp", "fsdp"), None),
        P(("dp", "fsdp"), None),
    )
    out_specs = P(("dp", "retr", "fsdp"), None)
    return jax.shard_map(body, mesh=mesh, in_specs=in_specs, out_specs=out_specs, check_vma=False)
```

profile of v0, /device:TPU:2, one launch (start us, length us, event | category | flops | bytes accessed | tf_op | source)
XLA Modules:
  0.0 400.2 jit_solution(17860496296428153999)
XLA Ops:
  6.5 0.0 all-gather.6.cloned.1.call-start
  6.5 0.7 all-gather.6.cloned.1.call-update
  7.3 0.0 all-gather.8.cloned.1.call-start
  7.3 0.7 all-gather.8.cloned.1.call-update
  8.0 0.0 all-gather.10.cloned.1.call-start
  8.1 0.7 all-gather.10.cloned.1.call-update
  8.7 0.7 multiply_add_fusion
  9.4 0.1 add.36
  9.5 0.1 add.34
  9.6 0.1 slice.14
  9.7 0.1 pad.4.clone
  9.8 1.4 maximum_bitcast_fusion
  11.2 1.1 copy.17
  12.3 53.7 %all-gather.6.cloned.1.call-done = bf16[32,128,896]{2,1,0:T(8,128)(2,1)} async-done(((bf16[4,128,896]{2,1,0:T(8,128)(2,1)}), bf16[32,128,896]{2,1,0:T(8,128)(2,1)}) %all-gather.6.cloned.1.call-update) | async-done | bytes 7340048 | tf_op jit(solution)/shard_map/all_gather | solution.py:26
  66.0 3.8 gather_fusion
  69.8 0.1 slice_select_fusion.1
  69.9 3.4 collective-permute-start
  73.3 0.1 broadcast_bitcast_fusion
  73.4 142.8 %all-gather.8.cloned.1.call-done = bf16[64,14,2048]{2,1,0:T(8,128)(2,1)} async-done(((bf16[1,14,2048]{2,1,0:T(8,128)(2,1)}), bf16[64,14,2048]{2,1,0:T(8,128)(2,1)}) %all-gather.8.cloned.1.call-update) | async-done | bytes 3670032 | tf_op jit(solution)/shard_map/all_gather | solution.py:32
  216.3 6.0 %reshape.73 = bf16[896,2048]{1,0:T(8,128)(2,1)} reshape(bf16[64,14,2048]{2,1,0:T(8,128)(2,1)} %all-gather.8.cloned.1.call-done) | data formatting | bytes 7340032
  222.2 137.9 %all-gather.10.cloned.1.call-done = bf16[64,14,2048]{2,1,0:T(8,128)(2,1)} async-done(((bf16[1,14,2048]{2,1,0:T(8,128)(2,1)}), bf16[64,14,2048]{2,1,0:T(8,128)(2,1)}) %all-gather.10.cloned.1.call-update) | async-done | bytes 3670032 | tf_op jit(solution)/shard_map/all_gather | solution.py:31
  360.1 6.0 %reshape.75 = bf16[896,2048]{1,0:T(8,128)(2,1)} reshape(bf16[64,14,2048]{2,1,0:T(8,128)(2,1)} %all-gather.10.cloned.1.call-done) | data formatting | bytes 7340032
  366.2 0.2 bitcast_select_fusion
  366.4 0.0 collective-permute-done
  366.4 6.0 %fusion.8 = bf16[96,8,16,128]{3,1,2,0:T(8,128)(2,1)S(1)} fusion(bf16[896,2048]{1,0:T(8,128)(2,1)} %reshape.73, bf16[512,896]{1,0:T(8,128)(2,1)S(1)} %bitcast_select_fusion, bf16[256,896]{1,0:T(8,128)(2,1)S(1)} %collective-permute-done), kind=kOutput, calls=%fused_computation.12 | convolution fusion | flops 2822897664 | bytes 8192000 | tf_op jit(solution)/shard_map/dot_general | solution.py:39
  372.5 0.0 copy-start
  372.5 2.7 copy.19
  375.1 0.0 copy-done
  375.2 4.0 fusion.9
  379.1 0.0 copy-start.1
  379.1 1.0 copy.18
  380.2 0.1 copy-done.1
  380.3 1.2 fusion.3
  381.5 1.1 fusion.30
  382.6 8.2 %fusion.15 = bf16[3,64,16,128]{3,1,2,0:T(8,128)(2,1)} fusion(bf16[3,256,16,128]{3,2,1,0:T(8,128)(2,1)} %bitcast.33, f32[3,16,64]{2,1,0:T(8,128)S(1)} %fusion.30, f32[3,16,64,256]{3,2,1,0:T(8,128)S(1)} %fusion.3), kind=kOutput, calls=%fused_computation.18 | convolution fusion | flops 205655296 | bytes 7090176 | tf_op jit(solution)/shard_map/chqk,ckhd->cqhd/dot_general | solution.py:59
  390.9 1.6 copy.16
  392.5 0.2 copy.32
  392.7 1.0 slice_select_fusion
  (6 shorter events, 0.0 us)
Async XLA Ops:
  6.5 59.5 %all-gather.6.cloned.1.call-start = ((), (), s32[]{:S(2)}) async-start(), calls=%async_computation | async-start | bytes 8257536 | tf_op jit(solution)/shard_map/all_gather | solution.py:26
  7.3 209.0 %all-gather.8.cloned.1.call-start = ((), (), s32[]{:S(2)}) async-start(), calls=%async_computation.1 | async-start | bytes 4259840 | tf_op jit(solution)/shard_map/all_gather | solution.py:32
  8.0 352.1 %all-gather.10.cloned.1.call-start = ((), (), s32[]{:S(2)}) async-start(), calls=%async_computation.2 | async-start | bytes 4259840 | tf_op jit(solution)/shard_map/all_gather | solution.py:31
  69.9 296.5 %collective-permute-start = (bf16[256,896]{1,0:T(8,128)(2,1)S(1)}, bf16[256,896]{1,0:T(8,128)(2,1)S(1)}, u32[]{:S(2)}, u32[]{:S(2)}) collective-permute-start(bf16[256,896]{1,0:T(8,128)(2,1)S(1)} %bitcast.36), channel_id=1, source_target_pairs={{0,1},{1,2},{2,3},{4,5},{5,6},{6,7},{8,9},{9,10},{10,11},{12,13},{... | collective-permute-start | bytes 1376264 | tf_op jit(solution)/shard_map/ppermute | solution.py:14
  372.5 2.7 copy-start
  379.1 1.1 copy-start.1
Sparse Core Ops, SparseCore 0:
  9.5 56.5 all-gather.5
  68.9 147.2 all-gather.7
  219.2 140.8 all-gather.9
where the time goes:
time: 401 us; the launch traced here: 400 us
  waiting for transfers between devices  337 us (84%)
  local copies, waits for them, and re-layouts  22.9 us (6%)
  matrix products  19.5 us (5%)
  between operations  13.2 us (3%)
  other arithmetic  4.63 us (1%)
    all_gather x1, waiting for transfers between devices, body(): lax.all_gather(value_weight, ('dp', 'fsdp'), axis=0, tiled=True)  143 us
    all_gather x1, waiting for transfers between devices, body(): lax.all_gather(key_weight, ('dp', 'fsdp'), axis=0, tiled=True)  138 us
    all_gather x1, waiting for transfers between devices, body(): gathered = lax.all_gather(encodings, 'retr', axis=0, tiled=True)  53.7 us
    unnamed x10, local copies, waits for them, and re-layouts  17.1 us
    dot_general x1, matrix products, body(): jnp.einsum('chqk,ckhd->cqhd', probs, value_heads, preferred_element_type=...  8.23 us
  transfers between devices with their start and end apart: 4, of which 3 were waited for; matrix products, arithmetic and copies ran while one was open for 5% of the time, Pallas kernels for 0%

commit v1 on v0

--- a/solution.py
+++ b/solution.py
@@ -6,6 +6,10 @@
 
 HEADS = 16
 STRETCH = 64
+loads_perform = lambda array_in: jnp.concatenate(
+    lax.all_to_all(jnp.stack([array_in] * lax.axis_size(("dp", "fsdp"))), ("dp", "fsdp"), 0, 0),
+    axis=0,
+)
 
 
 def passed_along(block, axis, distance):
@@ -29,7 +33,7 @@
     panel_rows = fetched.reshape(stretches * span, encodings.shape[2])
     key_full, value_full = (
         lax.all_gather(key_weight, ("dp", "fsdp"), axis=0, tiled=True),
-        lax.all_gather(value_weight, ("dp", "fsdp"), axis=0, tiled=True),
+        loads_perform(value_weight),
     )
     prior_rows = passed_along(panel_rows[(stretches - 1) * span :], "fsdp", 1)
     every_row = jnp.concatenate([prior_rows, panel_rows], 0)

time: 401 us -> 309 us (0.77)
  the two profiles are of different devices: /device:TPU:2 before, /device:TPU:16 now
where the time goes in v1:
time: 309 us; the launch traced here: 308 us
  waiting for transfers between devices  221 us (72%)
  local copies, waits for them, and re-layouts  27.2 us (9%)
  starting transfers between devices  22.1 us (7%)
  matrix products  21.5 us (7%)
  between operations  13.6 us (4%)
    all_gather x1, waiting for transfers between devices, body(): lax.all_gather(key_weight, ('dp', 'fsdp'), axis=0, tiled=True)  185 us
    all_gather x1, waiting for transfers between devices, body(): gathered = lax.all_gather(encodings, 'retr', axis=0, tiled=True)  34.5 us
    all_to_all x1, starting transfers between devices, lax.all_to_all(jnp.stack([array_in] * lax.axis_size(('dp', 'fsdp'))), ('d...  18.9 us
    unnamed x17, local copies, waits for them, and re-layouts  12 us
    dot_general x1, matrix products, body(): jnp.einsum('chqk,ckhd->cqhd', probs, value_heads, preferred_element_type=...  8.23 us
  transfers between devices with their start and end apart: 4, of which 2 were waited for; matrix products, arithmetic and copies ran while one was open for 8% of the time, Pallas kernels for 0%

profile of v1, /device:TPU:16, one launch (start us, length us, event | category | flops | bytes accessed | tf_op | source)
XLA Modules:
  0.0 308.2 jit_solution(9500217518601196052)
XLA Ops:
  6.5 0.0 all-gather.4.cloned.1.call-start
  6.5 0.7 all-gather.4.cloned.1.call-update
  7.3 3.4 %stack.2 = bf16[64,14,2048]{2,1,0:T(8,128)(2,1)} broadcast(bf16[14,2048]{1,0:T(8,128)(2,1)} %param.11), dimensions={1,2} | broadcast | bytes 3727360 | tf_op jit(solution)/shard_map/stack | solution.py:10
  10.7 0.0 copy-start.3
  10.7 0.0 copy-start.4
  10.7 0.0 copy-start.2
  10.7 18.9 %all-to-all-start = ((bf16[64,14,2048]{2,1,0:T(8,128)(2,1)}), bf16[64,14,2048]{2,1,0:T(8,128)(2,1)}, u32[]{:S(2)}, u32[]{:S(2)}) async-start(bf16[64,14,2048]{2,1,0:T(8,128)(2,1)} %stack.2), calls=%async_computation | async-start | bytes 8388608 | tf_op jit(solution)/shard_map/all_to_all | solution.py:10
  29.6 0.0 all-gather.6.cloned.1.call-start
  29.7 0.7 all-gather.6.cloned.1.call-update
  30.4 0.0 copy-done.3
  30.4 0.0 copy-done.4
  30.4 0.1 add.36
  30.5 0.1 add.34
  30.6 0.1 slice.14
  30.6 0.1 pad.4.clone
  30.7 0.0 copy-done.2
  30.7 0.4 maximum_bitcast_fusion
  31.1 1.1 copy.17
  32.2 34.5 %all-gather.4.cloned.1.call-done = bf16[32,128,896]{2,1,0:T(8,128)(2,1)} async-done(((bf16[4,128,896]{2,1,0:T(8,128)(2,1)}), bf16[32,128,896]{2,1,0:T(8,128)(2,1)}) %all-gather.4.cloned.1.call-update) | async-done | bytes 7340048 | tf_op jit(solution)/shard_map/all_gather | solution.py:30
  66.7 3.8 %gather_fusion = bf16[4,128,896]{2,1,0:T(8,128)(2,1)S(1)} fusion(bf16[32,128,896]{2,1,0:T(8,128)(2,1)} %all-gather.4.cloned.1.call-done, s32[1024]{0:T(1024)S(1)} %pad_clamp_fusion), kind=kCustom, calls=%fused_computation | custom fusion | bytes 1835024 | tf_op jit(solution)/shard_map/jit(_take)/gather | solution.py:31
  70.5 0.1 slice_select_fusion.1
  70.6 3.1 %collective-permute-start = (bf16[256,896]{1,0:T(8,128)(2,1)S(1)}, bf16[256,896]{1,0:T(8,128)(2,1)S(1)}, u32[]{:S(2)}, u32[]{:S(2)}) collective-permute-start(bf16[256,896]{1,0:T(8,128)(2,1)S(1)} %bitcast.35), channel_id=1, source_target_pairs={{0,1},{1,2},{2,3},{4,5},{5,6},{6,7},{8,9},{9,10},{10,11},{12,13},{... | collective-permute-start | bytes 1376264 | tf_op jit(solution)/shard_map/ppermute | solution.py:18
  73.7 0.1 broadcast_bitcast_fusion
  73.8 185.1 %all-gather.6.cloned.1.call-done = bf16[64,14,2048]{2,1,0:T(8,128)(2,1)} async-done(((bf16[1,14,2048]{2,1,0:T(8,128)(2,1)}), bf16[64,14,2048]{2,1,0:T(8,128)(2,1)}) %all-gather.6.cloned.1.call-update) | async-done | bytes 3670032 | tf_op jit(solution)/shard_map/all_gather | solution.py:35
  258.9 6.0 %reshape.79 = bf16[896,2048]{1,0:T(8,128)(2,1)} reshape(bf16[64,14,2048]{2,1,0:T(8,128)(2,1)} %all-gather.6.cloned.1.call-done) | data formatting | bytes 7340032
  264.9 0.2 bitcast_select_fusion
  265.1 0.0 copy-start.1
  265.1 0.0 collective-permute-done
  265.1 0.9 copy-done.1
  266.0 0.0 copy-start.5
  266.0 6.2 %fusion.9 = bf16[96,8,16,128]{3,1,2,0:T(8,128)(2,1)S(1)} fusion(bf16[896,2048]{1,0:T(8,128)(2,1)} %reshape.79, bf16[512,896]{1,0:T(8,128)(2,1)S(1)} %bitcast_select_fusion, bf16[256,896]{1,0:T(8,128)(2,1)S(1)} %collective-permute-done), kind=kOutput, calls=%fused_computation.13 | convolution fusion | flops 2822897664 | bytes 8192000 | tf_op jit(solution)/shard_map/dot_general | solution.py:40
  272.2 0.0 copy-done.5
  272.2 0.0 copy-start
  272.2 1.0 copy.18
  273.3 0.1 copy-done
  273.4 1.2 fusion.3
  274.6 1.1 fusion.30
  275.7 0.0 all-to-all-done
  275.7 6.0 %reshape.67 = bf16[896,2048]{1,0:T(8,128)(2,1)} reshape(bf16[64,14,2048]{2,1,0:T(8,128)(2,1)} %all-to-all-done) | data formatting | bytes 7340032 | tf_op jit(solution)/shard_map/reshape | solution.py:9
  281.7 5.9 %fusion.8 = bf16[96,8,16,128]{3,1,2,0:T(8,128)(2,1)S(1)} fusion(bf16[896,2048]{1,0:T(8,128)(2,1)} %reshape.67, bf16[512,896]{1,0:T(8,128)(2,1)} %copy-done.1, bf16[256,896]{1,0:T(8,128)(2,1)} %copy-done.5), kind=kOutput, calls=%fused_computation.12 | convolution fusion | flops 2822897664 | bytes 8192000 | tf_op jit(solution)/shard_map/dot_general | solution.py:43
  287.6 2.7 copy.19
  290.3 8.2 %fusion.15 = bf16[3,64,16,128]{3,1,2,0:T(8,128)(2,1)} fusion(bf16[3,256,16,128]{3,2,1,0:T(8,128)(2,1)} %bitcast.32, f32[3,16,64]{2,1,0:T(8,128)S(1)} %fusion.30, f32[3,16,64,256]{3,2,1,0:T(8,128)S(1)} %fusion.3), kind=kOutput, calls=%fused_computation.18 | convolution fusion | flops 205655296 | bytes 7090176 | tf_op jit(solution)/shard_map/chqk,ckhd->cqhd/dot_general | solution.py:63
  298.5 1.6 copy.16
  300.2 0.2 copy.32
  300.4 1.0 slice_select_fusion
  (7 shorter events, 0.0 us)
Async XLA Ops:
  6.5 60.1 %all-gather.4.cloned.1.call-start = ((), (), s32[]{:S(2)}) async-start(), calls=%async_computation.1 | async-start | bytes 8257536 | tf_op jit(solution)/shard_map/all_gather | solution.py:30
  10.7 19.7 %copy-start.3 = (s32[2,2]{1,0:T(2,128)S(1)}, s32[2,2]{1,0:T(2,128)}, u32[]{:S(2)}) copy-start(s32[2,2]{1,0:T(2,128)} %param.9) | copy-start | bytes 52
  10.7 19.7 %copy-start.4 = (s32[2,2]{1,0:T(2,128)S(1)}, s32[2,2]{1,0:T(2,128)}, u32[]{:S(2)}) copy-start(s32[2,2]{1,0:T(2,128)} %param.8) | copy-start | bytes 52
  10.7 20.1 %copy-start.2 = (bf16[128,2048]{1,0:T(8,128)(2,1)S(1)}, bf16[128,2048]{1,0:T(8,128)(2,1)}, u32[]{:S(2)}) copy-start(bf16[128,2048]{1,0:T(8,128)(2,1)} %param.6) | copy-start | bytes 1572868
  10.7 265.1 %all-to-all-start = ((bf16[64,14,2048]{2,1,0:T(8,128)(2,1)}), bf16[64,14,2048]{2,1,0:T(8,128)(2,1)}, u32[]{:S(2)}, u32[]{:S(2)}) async-start(bf16[64,14,2048]{2,1,0:T(8,128)(2,1)} %stack.2), calls=%async_computation | async-start | bytes 8388608 | tf_op jit(solution)/shard_map/all_to_all | solution.py:10
  29.6 229.3 %all-gather.6.cloned.1.call-start = ((), (), s32[]{:S(2)}) async-start(), calls=%async_computation.2 | async-start | bytes 4259840 | tf_op jit(solution)/shard_map/all_gather | solution.py:35
  70.6 194.5 %collective-permute-start = (bf16[256,896]{1,0:T(8,128)(2,1)S(1)}, bf16[256,896]{1,0:T(8,128)(2,1)S(1)}, u32[]{:S(2)}, u32[]{:S(2)}) collective-permute-start(bf16[256,896]{1,0:T(8,128)(2,1)S(1)} %bitcast.35), channel_id=1, source_target_pairs={{0,1},{1,2},{2,3},{4,5},{5,6},{6,7},{8,9},{9,10},{10,11},{12,13},{... | collective-permute-start | bytes 1376264 | tf_op jit(solution)/shard_map/ppermute | solution.py:18
  265.1 0.9 copy-start.1
  266.0 6.2 %copy-start.5 = (bf16[256,896]{1,0:T(8,128)(2,1)}, bf16[256,896]{1,0:T(8,128)(2,1)S(1)}, u32[]{:S(2)}) copy-start(bf16[256,896]{1,0:T(8,128)(2,1)S(1)} %collective-permute-done) | copy-start | bytes 1376260
  272.2 1.1 copy-start
Sparse Core Ops, SparseCore 0:
  9.5 57.1 all-gather.3
  69.6 189.2 all-gather.5
